TPU v7x, 128 devices: a whole 4x4x4 slice. The times are simulated.
128 devices in a mesh: section: 2 (over y_hi), fsdp: 8 (over z, core), replica: 8 (over x, y_lo).
Axes of the slice: x: 4, y: 4 (y_hi: 2, y_lo: 2; y = y_hi * 2 + y_lo), z: 4, core: 2. Of those that a mesh axis runs over, the one named last changes fastest.
Arguments:
- block_input: bfloat16 [8192, 1152], P(('fsdp', 'replica')), may hold values from -6 to 6
- out_cotangent: bfloat16 [8192, 1152], P(('fsdp', 'replica')), may hold values from -6 to 6
- seq_lengths: int32 [128], P(('fsdp', 'replica')), may hold values from 1 to 64, 5120 in all
- input_gain: bfloat16 [2, 1152], P('section', 'fsdp'), may hold values from 0.099609375 to 1.8984375
- query_weight: bfloat16 [2, 1152, 1024], P('section', 'fsdp'), may hold values from -0.1875 to 0.1875
- key_weight: bfloat16 [2, 1152, 256], P('section', 'fsdp'), may hold values from -0.1875 to 0.1875
- value_weight: bfloat16 [2, 1152, 256], P('section', 'fsdp'), may hold values from -0.1875 to 0.1875
- query_gain: bfloat16 [2, 256], P('section', 'fsdp'), may hold values from 0.099609375 to 1.8984375
- key_gain: bfloat16 [2, 256], P('section', 'fsdp'), may hold values from 0.099609375 to 1.8984375
- output_weight: bfloat16 [2, 1024, 1152], P('section', 'fsdp'), may hold values from -0.1875 to 0.1875
- attn_post_gain: bfloat16 [2, 1152], P('section', 'fsdp'), may hold values from 0.099609375 to 1.8984375
- ffw_pre_gain: bfloat16 [2, 1152], P('section', 'fsdp'), may hold values from 0.099609375 to 1.8984375
- gate_weight: bfloat16 [2, 1152, 6912], P('section', None, 'fsdp'), may hold values from -0.1875 to 0.1875
- up_weight: bfloat16 [2, 1152, 6912], P('section', None, 'fsdp'), may hold values from -0.1875 to 0.1875
- down_weight: bfloat16 [2, 6912, 1152], P('section', 'fsdp'), may hold values from -0.078125 to 0.078125
- ffw_post_gain: bfloat16 [2, 1152], P('section', 'fsdp'), may hold values from 0.099609375 to 1.8984375
Outputs:
- section_out: bfloat16 [2, 8192, 1152], P('section', ('fsdp', 'replica'))
- section_in_grad: bfloat16 [2, 8192, 1152], P('section', ('fsdp', 'replica'))
- input_gain_grad: float32 [2, 1152], P('section', 'fsdp')
- query_weight_grad: float32 [2, 1152, 1024], P('section', 'fsdp')
- key_weight_grad: float32 [2, 1152, 256], P('section', 'fsdp')
- value_weight_grad: float32 [2, 1152, 256], P('section', 'fsdp')
- query_gain_grad: float32 [2, 256], P('section', 'fsdp')
- key_gain_grad: float32 [2, 256], P('section', 'fsdp')
- output_weight_grad: float32 [2, 1024, 1152], P('section', 'fsdp')
- attn_post_gain_grad: float32 [2, 1152], P('section', 'fsdp')
- ffw_pre_gain_grad: float32 [2, 1152], P('section', 'fsdp')
- gate_weight_grad: float32 [2, 1152, 6912], P('section', None, 'fsdp')
- up_weight_grad: float32 [2, 1152, 6912], P('section', None, 'fsdp')
- down_weight_grad: float32 [2, 6912, 1152], P('section', 'fsdp')
- ffw_post_gain_grad: float32 [2, 1152], P('section', 'fsdp')
Inputs may be any that keep to these rules, and one draw needn't show every extreme that they name: `seq_lengths`: some sequence has exactly 64 live tokens.
All inputs are finite; a program needn't handle non-finite values. No bound on the sum of `seq_lengths` on one device may be relied on, other than what follows from the above.
Results may differ from a plain program's by a relative error of at most 0.029.
Values may be sent and summed in bfloat16 or wider, within the bound.
A program may use at most 256 MiB of HBM per device.

v0:
```python
import math

import jax
import jax.numpy as jnp
from jax import lax
from jax.sharding import PartitionSpec as P

D = 1152
HEADS = 4
HEAD = 256
MICRO = 2
SEQ_ROWS = 64


EPSILON = 1e-06
ROPE_BASE = 10000.0
GELU_CUBIC = 0.044715
GELU_SCALE = math.sqrt(2.0 / math.pi)


def shifted(shard, axis, by):
    devices = lax.axis_size(axis)
    pairs = [(i, i + by) for i in range(devices) if 0 <= i + by < devices]
    return lax.ppermute(shard, axis, pairs)


def norm_scale(values):
    return lax.rsqrt(jnp.mean(values * values, axis=-1, keepdims=True) + EPSILON)


def norm_back(values, gain_vector, grad_result):
    inverse_rms = norm_scale(values)
    scaled = grad_result * gain_vector
    grad_values = inverse_rms * scaled - values * inverse_rms**3 * jnp.mean(
        scaled * values, axis=-1, keepdims=True
    )
    gain_term = grad_result * values * inverse_rms
    return (grad_values, jnp.sum(gain_term.reshape(-1, gain_term.shape[-1]), axis=0))


def gelu_tanh(inputs):
    inner_arg = GELU_SCALE * (inputs + GELU_CUBIC * inputs**3)
    return 0.5 * inputs * (1.0 + jnp.tanh(inner_arg))


def gelu_slope(inputs):
    inner_arg = GELU_SCALE * (inputs + GELU_CUBIC * inputs**3)
    tangent = jnp.tanh(inner_arg)
    return 0.5 * (1.0 + tangent) + 0.5 * inputs * (1.0 - tangent * tangent) * GELU_SCALE * (
        1.0 + 3.0 * GELU_CUBIC * inputs * inputs
    )


def rope_tables(row_count, head_width):
    half_width = head_width // 2
    frequency = ROPE_BASE ** (-2.0 * jnp.arange(half_width, dtype=jnp.float32) / head_width)
    angles = jnp.arange(row_count, dtype=jnp.float32)[:, None] * frequency[None, :]
    return (jnp.cos(angles), jnp.sin(angles))


def rotate_pairs(vectors, cosine, sine_part):
    half_width = vectors.shape[-1] // 2
    first_half = vectors[..., :half_width]
    second_half = vectors[..., half_width:]
    return jnp.concatenate(
        [
            first_half * cosine - second_half * sine_part,
            second_half * cosine + first_half * sine_part,
        ],
        axis=-1,
    )


def attend_mask(lengths, row_count):
    position = jnp.arange(row_count, dtype=jnp.int32)
    causal = position[None, :] <= position[:, None]
    live_keys = position[None, :] < lengths[:, None]
    return causal[None, :, :] & live_keys[:, None, :]


def attend_scores(query_rot, key_rot):
    return jnp.einsum(
        "sihd,sjd->shij", query_rot.astype(jnp.float32), key_rot.astype(jnp.float32)
    ) * HEAD ** (-0.5)


def layer_forward(block_in, lengths, params):
    (
        input_gain,
        query_weight,
        key_weight,
        value_weight,
        query_gain,
        key_gain,
        output_weight,
        attn_post_gain,
        ffw_pre_gain,
        gate_weight,
        up_weight,
        down_weight,
        ffw_post_gain,
    ) = params
    seq_count, row_count, model_width = block_in.shape
    flat_rows = seq_count * row_count
    flat_in = block_in.reshape(flat_rows, model_width).astype(jnp.float32)
    normed_in = (flat_in * norm_scale(flat_in) * input_gain.astype(jnp.float32)).astype(
        jnp.bfloat16
    )
    query_raw = jnp.dot(normed_in, query_weight, preferred_element_type=jnp.float32).reshape(
        seq_count, row_count, HEADS, HEAD
    )
    key_raw = jnp.dot(normed_in, key_weight, preferred_element_type=jnp.float32).reshape(
        seq_count, row_count, HEAD
    )
    value_rows = (
        jnp.dot(normed_in, value_weight, preferred_element_type=jnp.float32)
        .astype(jnp.bfloat16)
        .reshape(seq_count, row_count, HEAD)
    )
    cosine, sine_part = rope_tables(row_count, HEAD)
    query_rot = rotate_pairs(
        query_raw * norm_scale(query_raw) * query_gain.astype(jnp.float32),
        cosine[:, None, :],
        sine_part[:, None, :],
    ).astype(jnp.bfloat16)
    key_rot = rotate_pairs(
        key_raw * norm_scale(key_raw) * key_gain.astype(jnp.float32), cosine, sine_part
    ).astype(jnp.bfloat16)
    allowed = attend_mask(lengths, row_count)[:, None, :, :]
    scores = attend_scores(query_rot, key_rot)
    exponent = jnp.where(allowed, jnp.exp(scores), 0.0)
    log_total = jnp.log(jnp.sum(exponent, axis=-1))
    probs = jnp.where(allowed, jnp.exp(scores - log_total[..., None]), 0.0)
    probs_b = probs.astype(jnp.bfloat16)
    context = jnp.einsum(
        "shij,sjd->sihd", probs_b.astype(jnp.float32), value_rows.astype(jnp.float32)
    )
    context_b = context.astype(jnp.bfloat16)
    attn_proj = jnp.dot(
        context_b.reshape(flat_rows, HEADS * HEAD),
        output_weight,
        preferred_element_type=jnp.float32,
    )
    hidden = flat_in + attn_proj * norm_scale(attn_proj) * attn_post_gain.astype(jnp.float32)
    normed_mid = (hidden * norm_scale(hidden) * ffw_pre_gain.astype(jnp.float32)).astype(
        jnp.bfloat16
    )
    gate_rows = jnp.dot(normed_mid, gate_weight, preferred_element_type=jnp.float32)
    up_rows = jnp.dot(normed_mid, up_weight, preferred_element_type=jnp.float32)
    mixed = (gelu_tanh(gate_rows) * up_rows).astype(jnp.bfloat16)
    ffw_proj = jnp.dot(mixed, down_weight, preferred_element_type=jnp.float32)
    block_out = (
        hidden + ffw_proj * norm_scale(ffw_proj) * ffw_post_gain.astype(jnp.float32)
    ).astype(jnp.bfloat16)
    saved = (
        flat_in,
        normed_in,
        query_raw,
        key_raw,
        query_rot,
        key_rot,
        value_rows,
        log_total,
        context,
        context_b,
        attn_proj,
        hidden,
        normed_mid,
        gate_rows,
        up_rows,
        mixed,
        ffw_proj,
    )
    return (block_out.reshape(seq_count, row_count, model_width), saved)


def layer_backward(grad_result, lengths, params, saved):
    (
        input_gain,
        query_weight,
        key_weight,
        value_weight,
        query_gain,
        key_gain,
        output_weight,
        attn_post_gain,
        ffw_pre_gain,
        gate_weight,
        up_weight,
        down_weight,
        ffw_post_gain,
    ) = params
    (
        flat_in,
        normed_in,
        query_raw,
        key_raw,
        query_rot,
        key_rot,
        value_rows,
        log_total,
        context,
        context_b,
        attn_proj,
        hidden,
        normed_mid,
        gate_rows,
        up_rows,
        mixed,
        ffw_proj,
    ) = saved
    seq_count, row_count = (query_raw.shape[0], query_raw.shape[1])
    flat_rows = seq_count * row_count
    grad_ffw, sum_ffw_post = norm_back(ffw_proj, ffw_post_gain.astype(jnp.float32), grad_result)
    grad_ffw_b = grad_ffw.astype(jnp.bfloat16)
    grad_mixed = jnp.dot(grad_ffw_b, down_weight.T, preferred_element_type=jnp.float32)
    grad_gate_b = (grad_mixed * up_rows * gelu_slope(gate_rows)).astype(jnp.bfloat16)
    grad_up_b = (grad_mixed * gelu_tanh(gate_rows)).astype(jnp.bfloat16)
    grad_mid = jnp.dot(grad_gate_b, gate_weight.T, preferred_element_type=jnp.float32) + jnp.dot(
        grad_up_b, up_weight.T, preferred_element_type=jnp.float32
    )
    grad_hidden_part, sum_ffw_pre = norm_back(hidden, ffw_pre_gain.astype(jnp.float32), grad_mid)
    grad_hidden = grad_result + grad_hidden_part
    grad_attn, sum_attn_post = norm_back(attn_proj, attn_post_gain.astype(jnp.float32), grad_hidden)
    grad_attn_b = grad_attn.astype(jnp.bfloat16)
    grad_context_b = (
        jnp.dot(grad_attn_b, output_weight.T, preferred_element_type=jnp.float32)
        .astype(jnp.bfloat16)
        .reshape(seq_count, row_count, HEADS, HEAD)
    )
    allowed = attend_mask(lengths, row_count)[:, None, :, :]
    scores = attend_scores(query_rot, key_rot)
    probs = jnp.where(allowed, jnp.exp(scores - log_total[..., None]), 0.0)
    probs_b = probs.astype(jnp.bfloat16)
    grad_value = jnp.einsum(
        "shij,sihd->sjd", probs_b.astype(jnp.float32), grad_context_b.astype(jnp.float32)
    )
    grad_probs = jnp.einsum(
        "sihd,sjd->shij", grad_context_b.astype(jnp.float32), value_rows.astype(jnp.float32)
    )
    row_delta = jnp.transpose(
        jnp.sum(grad_context_b.astype(jnp.float32) * context, axis=-1), (0, 2, 1)
    )
    grad_scores = (probs * (grad_probs - row_delta[..., None]) * HEAD ** (-0.5)).astype(
        jnp.bfloat16
    )
    grad_query_rot = jnp.einsum(
        "shij,sjd->sihd", grad_scores.astype(jnp.float32), key_rot.astype(jnp.float32)
    )
    grad_key_rot = jnp.einsum(
        "shij,sihd->sjd", grad_scores.astype(jnp.float32), query_rot.astype(jnp.float32)
    )
    cosine, sine_part = rope_tables(row_count, HEAD)
    grad_query_norm = rotate_pairs(grad_query_rot, cosine[:, None, :], -sine_part[:, None, :])
    grad_key_norm = rotate_pairs(grad_key_rot, cosine, -sine_part)
    grad_query, sum_query = norm_back(query_raw, query_gain.astype(jnp.float32), grad_query_norm)
    grad_key, sum_key = norm_back(key_raw, key_gain.astype(jnp.float32), grad_key_norm)
    grad_query_b = grad_query.astype(jnp.bfloat16).reshape(flat_rows, HEADS * HEAD)
    grad_key_b = grad_key.astype(jnp.bfloat16).reshape(flat_rows, HEAD)
    grad_value_b = grad_value.astype(jnp.bfloat16).reshape(flat_rows, HEAD)
    grad_normed = (
        jnp.dot(grad_query_b, query_weight.T, preferred_element_type=jnp.float32)
        + jnp.dot(grad_key_b, key_weight.T, preferred_element_type=jnp.float32)
        + jnp.dot(grad_value_b, value_weight.T, preferred_element_type=jnp.float32)
    )
    grad_in_part, sum_input = norm_back(flat_in, input_gain.astype(jnp.float32), grad_normed)
    grad_in = grad_hidden + grad_in_part
    parts = (
        sum_input,
        normed_in,
        grad_query_b,
        grad_key_b,
        grad_value_b,
        sum_query,
        sum_key,
        context_b.reshape(flat_rows, HEADS * HEAD),
        grad_attn_b,
        sum_attn_post,
        sum_ffw_pre,
        normed_mid,
        grad_gate_b,
        grad_up_b,
        mixed,
        grad_ffw_b,
        sum_ffw_post,
    )
    return (grad_in, parts)


def outer_sum(left_rows, right_rows):
    return lax.dot_general(
        left_rows, right_rows, (((0,), (0,)), ((), ())), preferred_element_type=jnp.float32
    )


def own_columns(rows_array, fsdp_count, fsdp_index):
    width = rows_array.shape[1] // fsdp_count
    return lax.dynamic_slice_in_dim(rows_array, fsdp_index * width, width, 1)


def shards(
    block_input,
    out_cotangent,
    seq_lengths,
    input_gain,
    query_weight,
    key_weight,
    value_weight,
    query_gain,
    key_gain,
    output_weight,
    attn_post_gain,
    ffw_pre_gain,
    gate_weight,
    up_weight,
    down_weight,
    ffw_post_gain,
):
    section_index = lax.axis_index("section")
    gathered = (
        lax.all_gather(input_gain, "fsdp", axis=1, tiled=True),
        lax.all_gather(query_weight, "fsdp", axis=1, tiled=True),
        lax.all_gather(key_weight, "fsdp", axis=1, tiled=True),
        lax.all_gather(value_weight, "fsdp", axis=1, tiled=True),
        lax.all_gather(query_gain, "fsdp", axis=1, tiled=True),
        lax.all_gather(key_gain, "fsdp", axis=1, tiled=True),
        lax.all_gather(output_weight, "fsdp", axis=1, tiled=True),
        lax.all_gather(attn_post_gain, "fsdp", axis=1, tiled=True),
        lax.all_gather(ffw_pre_gain, "fsdp", axis=1, tiled=True),
        lax.all_gather(gate_weight, "fsdp", axis=2, tiled=True),
        lax.all_gather(up_weight, "fsdp", axis=2, tiled=True),
        lax.all_gather(down_weight, "fsdp", axis=1, tiled=True),
        lax.all_gather(ffw_post_gain, "fsdp", axis=1, tiled=True),
    )
    params = tuple((full_param[0] for full_param in gathered))
    micro_inputs = block_input.reshape(MICRO, SEQ_ROWS, D)
    micro_cotangents = out_cotangent.reshape(MICRO, SEQ_ROWS, D)
    received = jnp.zeros((1, SEQ_ROWS, D), jnp.bfloat16)
    forward_outs = []
    forward_saved = []
    for tick_index in range(MICRO + 1):
        own_rows = micro_inputs[min(tick_index, MICRO - 1)][None]
        current = jnp.where(section_index == 0, own_rows, received)
        micro_index = jnp.clip(tick_index - section_index, 0, MICRO - 1)
        lengths = lax.dynamic_slice_in_dim(seq_lengths, micro_index, 1)
        block_out, saved = layer_forward(current, lengths, params)
        forward_outs.append(block_out)
        forward_saved.append(saved)
        if tick_index < MICRO:
            received = shifted(block_out, "section", 1)
    section_out = lax.dynamic_slice_in_dim(
        jnp.stack(forward_outs), section_index, MICRO, 0
    ).reshape(1, MICRO * SEQ_ROWS, D)
    position = jnp.arange(SEQ_ROWS, dtype=jnp.int32)
    received_grad = jnp.zeros((SEQ_ROWS, D), jnp.bfloat16)
    grads_sent = []
    parts_list = []
    for tick_index in range(MICRO + 1):
        late_micro = max(MICRO - 1 - tick_index, 0)
        early_micro = min(MICRO - tick_index, MICRO - 1)
        micro_index = jnp.where(section_index == 1, late_micro, early_micro).astype(jnp.int32)
        lengths = lax.dynamic_slice_in_dim(seq_lengths, micro_index, 1)
        live_rows = (position < lengths[0]).astype(jnp.float32)[:, None]
        top_grad = micro_cotangents[late_micro].astype(jnp.float32) * live_rows
        grad_result = jnp.where(section_index == 1, top_grad, received_grad.astype(jnp.float32))
        grad_in, parts = layer_backward(
            grad_result, lengths, params, forward_saved[MICRO - tick_index]
        )
        grad_in_b = grad_in.astype(jnp.bfloat16)
        grads_sent.append(grad_in_b)
        parts_list.append(parts)
        if tick_index < MICRO:
            received_grad = shifted(grad_in_b, "section", -1)
    first_useful = 1 - section_index
    useful_grads = lax.dynamic_slice_in_dim(jnp.stack(grads_sent), first_useful, MICRO, 0)
    section_in_grad = jnp.flip(useful_grads, axis=0).reshape(1, MICRO * SEQ_ROWS, D)
    selected = []
    for part_index in range(len(parts_list[0])):
        stacked_part = jnp.stack([tick_parts[part_index] for tick_parts in parts_list])
        useful_part = lax.dynamic_slice_in_dim(stacked_part, first_useful, MICRO, 0)
        if useful_part.ndim == 2:
            selected.append(jnp.sum(useful_part, axis=0))
        else:
            selected.append(useful_part.reshape(MICRO * useful_part.shape[1], useful_part.shape[2]))
    (
        sum_input,
        normed_rows,
        grad_query_b,
        grad_key_b,
        grad_value_b,
        sum_query,
        sum_key,
        context_rows,
        grad_attn_b,
        sum_attn_post,
        sum_ffw_pre,
        normed_mid,
        grad_gate_b,
        grad_up_b,
        mixed,
        grad_ffw_b,
        sum_ffw_post,
    ) = tuple(selected)
    gain_shards = (
        lax.psum_scatter(sum_input, "fsdp", scatter_dimension=0, tiled=True),
        lax.psum_scatter(sum_query, "fsdp", scatter_dimension=0, tiled=True),
        lax.psum_scatter(sum_key, "fsdp", scatter_dimension=0, tiled=True),
        lax.psum_scatter(sum_attn_post, "fsdp", scatter_dimension=0, tiled=True),
        lax.psum_scatter(sum_ffw_pre, "fsdp", scatter_dimension=0, tiled=True),
        lax.psum_scatter(sum_ffw_post, "fsdp", scatter_dimension=0, tiled=True),
    )
    fsdp_count = lax.axis_size("fsdp")
    fsdp_index = lax.axis_index("fsdp")
    gathered_rows = (
        lax.all_gather(normed_rows, "fsdp", axis=0, tiled=True),
        lax.all_gather(context_rows, "fsdp", axis=0, tiled=True),
        lax.all_gather(mixed, "fsdp", axis=0, tiled=True),
        lax.all_gather(grad_gate_b, "fsdp", axis=0, tiled=True),
        lax.all_gather(grad_up_b, "fsdp", axis=0, tiled=True),
        lax.all_gather(grad_query_b, "fsdp", axis=0, tiled=True),
        lax.all_gather(grad_key_b, "fsdp", axis=0, tiled=True),
        lax.all_gather(grad_value_b, "fsdp", axis=0, tiled=True),
        lax.all_gather(grad_attn_b, "fsdp", axis=0, tiled=True),
        lax.all_gather(normed_mid, "fsdp", axis=0, tiled=True),
        lax.all_gather(grad_ffw_b, "fsdp", axis=0, tiled=True),
    )
    own_parts = tuple(
        (own_columns(rows_array, fsdp_count, fsdp_index) for rows_array in gathered_rows[:5])
    )
    full_parts = gathered_rows[5:]
    normed_own, context_own, mixed_own, gate_own, up_own = own_parts
    query_all, key_all, value_all, attn_all, normed_mid_all, ffw_all = full_parts
    query_shard = outer_sum(normed_own, query_all)
    key_shard = outer_sum(normed_own, key_all)
    value_shard = outer_sum(normed_own, value_all)
    output_shard = outer_sum(context_own, attn_all)
    gate_shard = outer_sum(normed_mid_all, gate_own)
    up_shard = outer_sum(normed_mid_all, up_own)
    down_shard = outer_sum(mixed_own, ffw_all)
    totals = (
        lax.psum(gain_shards[0].astype(jnp.bfloat16), "replica").astype(jnp.float32),
        lax.psum(query_shard.astype(jnp.bfloat16), "replica").astype(jnp.float32),
        lax.psum(key_shard.astype(jnp.bfloat16), "replica").astype(jnp.float32),
        lax.psum(value_shard.astype(jnp.bfloat16), "replica").astype(jnp.float32),
        lax.psum(gain_shards[1].astype(jnp.bfloat16), "replica").astype(jnp.float32),
        lax.psum(gain_shards[2].astype(jnp.bfloat16), "replica").astype(jnp.float32),
        lax.psum(output_shard.astype(jnp.bfloat16), "replica").astype(jnp.float32),
        lax.psum(gain_shards[3].astype(jnp.bfloat16), "replica").astype(jnp.float32),
        lax.psum(gain_shards[4].astype(jnp.bfloat16), "replica").astype(jnp.float32),
        lax.psum(gate_shard.astype(jnp.bfloat16), "replica").astype(jnp.float32),
        lax.psum(up_shard.astype(jnp.bfloat16), "replica").astype(jnp.float32),
        lax.psum(down_shard.astype(jnp.bfloat16), "replica").astype(jnp.float32),
        lax.psum(gain_shards[5].astype(jnp.bfloat16), "replica").astype(jnp.float32),
    )
    return (
        section_out,
        section_in_grad,
        totals[0][None],
        totals[1][None],
        totals[2][None],
        totals[3][None],
        totals[4][None],
        totals[5][None],
        totals[6][None],
        totals[7][None],
        totals[8][None],
        totals[9][None],
        totals[10][None],
        totals[11][None],
        totals[12][None],
    )


def solution(mesh):
    placed = (
        P(("fsdp", "replica"), None),
        P(("fsdp", "replica"), None),
        P(("fsdp", "replica")),
        P("section", "fsdp"),
        P("section", "fsdp", None),
        P("section", "fsdp", None),
        P("section", "fsdp", None),
        P("section", "fsdp"),
        P("section", "fsdp"),
        P("section", "fsdp", None),
        P("section", "fsdp"),
        P("section", "fsdp"),
        P("section", None, "fsdp"),
        P("section", None, "fsdp"),
        P("section", "fsdp", None),
        P("section", "fsdp"),
    )
    return jax.shard_map(
        shards,
        mesh=mesh,
        in_specs=placed,
        out_specs=(
            P("section", ("fsdp", "replica"), None),
            P("section", ("fsdp", "replica"), None),
            P("section", "fsdp"),
            P("section", "fsdp", None),
            P("section", "fsdp", None),
            P("section", "fsdp", None),
            P("section", "fsdp"),
            P("section", "fsdp"),
            P("section", "fsdp", None),
            P("section", "fsdp"),
            P("section", "fsdp"),
            P("section", None, "fsdp"),
            P("section", None, "fsdp"),
            P("section", "fsdp", None),
            P("section", "fsdp"),
        ),
        check_vma=False,
    )
```

profile of v0, /device:TPU:7, one launch (start us, length us, event | category | flops | bytes accessed | tf_op | source)
XLA Modules:
  0.0 1355.5 jit_solution(9772724777270850052)
XLA Ops:
  14.2 24.9 %all-reduce.15 = (bf16[1152]{0:T(1024)(128)(2,1)S(1)}, bf16[256]{0:T(256)(128)(2,1)S(1)}, bf16[256]{0:T(256)(128)(2,1)S(1)}, bf16[1152]{0:T(1024)(128)(2,1)S(1)}...) all-reduce(bf16[1152]{0:T(1024)(128)(2,1)S(1)} %dynamic-update-slic, ...), channel_id=1, replica_groups=mesh['section'=2,'fsdp'=8,'replica'=8] {'fsdp'}, use_global_device_ids=true, to_apply=%add | all-reduce | flops 5120 | bytes 20480
  44.3 17.3 %all_gather.73 = bf16[1,1152,256]{2,1,0:T(8,128)(2,1)S(1)} all-gather(bf16[1,144,256]{2,1,0:T(8,128)(2,1)S(1)} %copy-done.163), channel_id=1, replica_groups=mesh['section'=2,'fsdp'=8,'replica'=8] {'fsdp'}, dimensions={1}, use_global_device_ids=true | all-gather | bytes 663552 | tf_op jit(solution)/shard_map/all_gather | solution.py:324
  61.9 13.4 all_gather.74
  80.3 2.6 fusion.61
  85.9 2.3 multiply_reduce_fusion.26
  89.7 61.2 %all-gather.19.cloned.1.call-done = bf16[1,1152,6912]{1,2,0:T(8,128)(2,1)} async-done(((bf16[1,1152,864]{1,2,0:T(8,128)(2,1)}), bf16[1,1152,6912]{1,2,0:T(8,128)(2,1)}) %all-gather.19.cloned.1.call-update) | async-done | bytes 15925264 | tf_op jit(solution)/shard_map/all_gather | solution.py:330
  150.9 10.2 fusion.34
  161.1 73.3 %all-gather.21.cloned.1.call-done = bf16[1,1152,6912]{1,2,0:T(8,128)(2,1)} async-done(((bf16[1,1152,864]{1,2,0:T(8,128)(2,1)}), bf16[1,1152,6912]{1,2,0:T(8,128)(2,1)}) %all-gather.21.cloned.1.call-update) | async-done | bytes 15925264 | tf_op jit(solution)/shard_map/all_gather | solution.py:331
  234.4 11.7 multiply_convert_fusion.5
  246.2 71.8 %all-gather.23.cloned.1.call-done = bf16[1,6912,1152]{2,1,0:T(8,128)(2,1)} async-done(((bf16[1,864,1152]{2,1,0:T(8,128)(2,1)}), bf16[1,6912,1152]{2,1,0:T(8,128)(2,1)}) %all-gather.23.cloned.1.call-update) | async-done | bytes 15925264 | tf_op jit(solution)/shard_map/all_gather | solution.py:332
  317.9 8.8 multiply_reduce_fusion.24
  328.0 5.0 collective-permute-start
  333.8 1.8 collective-permute-done
  355.5 11.4 fusion.32
  367.0 12.3 multiply_convert_fusion.4
  379.2 8.8 multiply_reduce_fusion.21
  389.2 5.8 collective-permute-start.1
  416.9 1.8 fusion.365
  418.8 2.3 multiply_reduce_fusion.20
  423.4 11.5 fusion.30
  434.8 12.3 multiply_convert_fusion.3
  447.2 8.8 multiply_reduce_fusion.18
  457.7 12.7 fusion.92
  470.4 8.7 fusion.16
  479.2 9.2 multiply_reduce_fusion.5
  498.9 1.8 fusion.139
  527.7 12.5 fusion.97
  540.2 8.7 fusion.14
  549.0 9.2 multiply_reduce_fusion.4
  569.7 1.8 fusion.140
  590.2 1.8 multiply_reduce_fusion
  593.8 12.5 fusion.102
  606.2 8.7 fusion.12
  615.0 9.2 multiply_reduce_fusion.3
  635.7 1.8 fusion.141
  650.1 1.8 fusion.221
  653.0 2.2 fusion.104
  657.2 3.3 fusion.108
  662.1 3.4 fusion.106
  666.3 16.0 %all_gather.87 = bf16[1024,256]{1,0:T(8,128)(2,1)S(1)} all-gather(bf16[128,256]{1,0:T(8,128)(2,1)S(1)} %bitcast.731), channel_id=1, replica_groups=mesh['section'=2,'fsdp'=8,'replica'=8] {'fsdp'}, dimensions={0}, use_global_device_ids=true | all-gather | bytes 589824 | tf_op jit(solution)/shard_map/all_gather | solution.py:421
  682.2 13.8 %all_gather.88 = bf16[1024,256]{1,0:T(8,128)(2,1)S(1)} all-gather(bf16[128,256]{1,0:T(8,128)(2,1)S(1)} %bitcast.732), channel_id=1, replica_groups=mesh['section'=2,'fsdp'=8,'replica'=8] {'fsdp'}, dimensions={0}, use_global_device_ids=true | all-gather | bytes 589824 | tf_op jit(solution)/shard_map/all_gather | solution.py:422
  696.1 2.3 fusion.134
  698.4 2.3 fusion.135
  700.7 5.4 all-gather.29.cloned.1.call-done
  706.2 28.0 %all-gather.31.cloned.1.call-done = bf16[1024,1152]{1,0:T(8,128)(2,1)} async-done(((bf16[128,1152]{1,0:T(8,128)(2,1)}), bf16[1024,1152]{1,0:T(8,128)(2,1)}) %all-gather.31.cloned.1.call-update) | async-done | bytes 2359312 | tf_op jit(solution)/shard_map/all_gather | solution.py:423
  734.2 3.0 fusion.72
  737.2 24.7 %all-gather.27.cloned.1.call-done = bf16[1024,1024]{1,0:T(8,128)(2,1)} async-done(((bf16[128,1024]{1,0:T(8,128)(2,1)}), bf16[1024,1024]{1,0:T(8,128)(2,1)}) %all-gather.27.cloned.1.call-update) | async-done | bytes 2097168 | tf_op jit(solution)/shard_map/all_gather | solution.py:420
  761.9 3.3 fusion.109
  765.2 24.3 %all-gather.41.cloned.1.call-done = bf16[1024,1152]{1,0:T(8,128)(2,1)} async-done(((bf16[128,1152]{1,0:T(8,128)(2,1)}), bf16[1024,1152]{1,0:T(8,128)(2,1)}) %all-gather.41.cloned.1.call-update) | async-done | bytes 2359312 | tf_op jit(solution)/shard_map/all_gather | solution.py:425
  789.5 76.9 %all-gather.39.cloned.1.call-done = bf16[1024,6912]{1,0:T(8,128)(2,1)} async-done(((bf16[128,6912]{1,0:T(8,128)(2,1)}), bf16[1024,6912]{1,0:T(8,128)(2,1)}) %all-gather.39.cloned.1.call-update) | async-done | bytes 14155792 | tf_op jit(solution)/shard_map/all_gather | solution.py:417
  866.4 6.5 fusion.38
  872.9 21.2 %all-gather.33.cloned.1.call-done = bf16[1024,1152]{1,0:T(8,128)(2,1)} async-done(((bf16[128,1152]{1,0:T(8,128)(2,1)}), bf16[1024,1152]{1,0:T(8,128)(2,1)}) %all-gather.33.cloned.1.call-update) | async-done | bytes 2359312 | tf_op jit(solution)/shard_map/all_gather | solution.py:424
  894.1 76.9 %all-gather.35.cloned.1.call-done = bf16[1024,6912]{1,0:T(8,128)(2,1)} async-done(((bf16[128,6912]{1,0:T(8,128)(2,1)}), bf16[1024,6912]{1,0:T(8,128)(2,1)}) %all-gather.35.cloned.1.call-update) | async-done | bytes 14155792 | tf_op jit(solution)/shard_map/all_gather | solution.py:418
  971.0 6.5 fusion.36
  977.4 70.1 %all-gather.37.cloned.1.call-done = bf16[1024,6912]{1,0:T(8,128)(2,1)} async-done(((bf16[128,6912]{1,0:T(8,128)(2,1)}), bf16[1024,6912]{1,0:T(8,128)(2,1)}) %all-gather.37.cloned.1.call-update) | async-done | bytes 14155792 | tf_op jit(solution)/shard_map/all_gather | solution.py:419
  1047.5 5.8 fusion.37
  1060.4 22.2 %all-reduce.12 = (bf16[1152]{0:T(1024)(128)(2,1)S(1)}, bf16[256]{0:T(256)(128)(2,1)S(1)}, bf16[256]{0:T(256)(128)(2,1)S(1)}, bf16[1152]{0:T(1024)(128)(2,1)S(1)}...) all-reduce(f32[1152]{0:T(1024)S(1)} %get-tuple-element.212, ...), channel_id=2, replica_groups=mesh['section'=2,'fsdp'=8,'replica'=8] {'fsdp'}, use_global_device_ids=true, to_apply=%region_46.47.clone | all-reduce | flops 5120 | bytes 30720
  1083.0 18.7 %all-reduce.13 = (bf16[1,144]{1,0:T(2,128)(2,1)S(1)}, bf16[1,32]{1,0:T(2,128)(2,1)S(1)}, bf16[1,32]{1,0:T(2,128)(2,1)S(1)}, bf16[1,144]{1,0:T(2,128)(2,1)S(1)}, ...) all-reduce(bf16[1,144]{1,0:T(2,128)(2,1)S(1)} %broadcast_in_dim.132, ...), channel_id=1, replica_groups=mesh['section'=2,'fsdp'=8,'replica'=8] {'replica'}, use_global_device_ids=true, to_apply=%region_47.48 | all-reduce | flops 640 | bytes 2560 | tf_op jit(solution)/shard_map/psum | solution.py:441
  1105.0 229.7 %all-reduce.18.cloned.1.call-done = (bf16[1,144,1024]{2,1,0:T(8,128)(2,1)}, bf16[1,144,256]{2,1,0:T(8,128)(2,1)}, bf16[1,144,256]{2,1,0:T(8,128)(2,1)}, bf16[1,1...) async-done(((bf16[1,144,1024]{2,1,0:T(8,128)(2,1)}, bf16[1,144,256]{2,1,0:T(8,128)(2,1)}, ...) | async-done | bytes 6709264 | tf_op jit(solution)/shard_map/psum | solution.py:442
  1334.7 2.0 broadcast_in_dim.135
  1339.8 1.8 broadcast_in_dim.145
  1341.6 2.2 broadcast_in_dim.151
  1344.0 2.2 broadcast_in_dim.153
  1346.3 2.2 broadcast_in_dim.155
  (885 shorter events, 178.3 us)
Async XLA Ops:
  7.2 73.0 %all-gather.15.cloned.1.call-start = ((), (), s32[]{:S(2)}) async-start(), calls=%async_computation | async-start | bytes 2654208 | tf_op jit(solution)/shard_map/all_gather | solution.py:322
  7.9 78.0 %all-gather.17.cloned.1.call-start = ((), (), s32[]{:S(2)}) async-start(), calls=%async_computation.1 | async-start | bytes 2654208 | tf_op jit(solution)/shard_map/all_gather | solution.py:327
  8.7 142.2 %all-gather.19.cloned.1.call-start = ((), (), s32[]{:S(2)}) async-start(), calls=%async_computation.2 | async-start | bytes 17915904 | tf_op jit(solution)/shard_map/all_gather | solution.py:330
  9.5 29.7 %copy-start.217 = (s32[2]{0:T(128)S(1)}, s32[2]{0:T(128)}, u32[]{:S(2)}) copy-start(s32[2]{0:T(128)} %param.18) | copy-start | bytes 28
  9.5 34.1 %copy-start.64 = (bf16[128,1152]{1,0:T(8,128)(2,1)S(1)}, bf16[128,1152]{1,0:T(8,128)(2,1)}, u32[]{:S(2)}) copy-start(bf16[128,1152]{1,0:T(8,128)(2,1)} %param.16) | copy-start | bytes 884740
  9.5 34.8 %copy-start.163 = (bf16[1,144,256]{2,1,0:T(8,128)(2,1)S(1)}, bf16[1,144,256]{2,1,0:T(8,128)(2,1)}, u32[]{:S(2)}) copy-start(bf16[1,144,256]{2,1,0:T(8,128)(2,1)} %param.22) | copy-start | bytes 221188
  9.5 224.9 %all-gather.21.cloned.1.call-start = ((), (), s32[]{:S(2)}) async-start(), calls=%async_computation.3 | async-start | bytes 17915904 | tf_op jit(solution)/shard_map/all_gather | solution.py:331
  10.1 51.8 %copy-start.164 = (bf16[1,144,256]{2,1,0:T(8,128)(2,1)S(1)}, bf16[1,144,256]{2,1,0:T(8,128)(2,1)}, u32[]{:S(2)}) copy-start(bf16[1,144,256]{2,1,0:T(8,128)(2,1)} %param.21) | copy-start | bytes 221188
  10.1 307.8 %all-gather.23.cloned.1.call-start = ((), (), s32[]{:S(2)}) async-start(), calls=%async_computation.4 | async-start | bytes 17915904 | tf_op jit(solution)/shard_map/all_gather | solution.py:332
  10.7 685.4 %all-gather.25.cloned.1.call-start = ((), (), s32[]{:S(2)}) async-start(), calls=%async_computation.5 | async-start | bytes 2654208 | tf_op jit(solution)/shard_map/all_gather | solution.py:415
  39.1 49.8 %copy-start.120 = (f32[1152]{0:T(1024)}, f32[1152]{0:T(1024)S(1)}, u32[]{:S(2)}) copy-start(f32[1152]{0:T(1024)S(1)} %mul.2664) | copy-start | bytes 13828
  39.1 41.1 %copy-start.126 = (f32[1152]{0:T(1024)}, f32[1152]{0:T(1024)S(1)}, u32[]{:S(2)}) copy-start(f32[1152]{0:T(1024)S(1)} %mul.2663) | copy-start | bytes 13828
  39.1 44.7 %copy-start.183 = (f32[256]{0:T(256)}, f32[256]{0:T(256)S(1)}, u32[]{:S(2)}) copy-start(f32[256]{0:T(256)S(1)} %convert_element_type.623) | copy-start | bytes 3076
  39.1 41.1 %copy-start.159 = (f32[256]{0:T(256)}, f32[256]{0:T(256)S(1)}, u32[]{:S(2)}) copy-start(f32[256]{0:T(256)S(1)} %convert_element_type.622) | copy-start | bytes 3076
  39.2 41.0 %copy-start.201 = (f32[128]{0:T(128)}, f32[128]{0:T(128)S(1)}, u32[]{:S(2)}) copy-start(f32[128]{0:T(128)S(1)} %multiply_power_fusion) | copy-start | bytes 1540
  44.3 36.0 %copy-start.227 = (f32[64]{0:T(128)}, f32[64]{0:T(128)S(1)}, u32[]{:S(2)}) copy-start(f32[64]{0:T(128)S(1)} %get-tuple-element.132) | copy-start | bytes 772
  61.9 22.9 %copy-start.200 = (bf16[64,256,1]{1,0,2:T(8,128)(2,1)}, bf16[64,256,1]{1,0,2:T(8,128)(2,1)S(1)}, u32[]{:S(2)}) copy-start(bf16[64,256,1]{1,0,2:T(8,128)(2,1)S(1)} %fusion.142) | copy-start | bytes 98308
  88.2 72.8 %copy-start.37 = (f32[64,1152]{1,0:T(8,128)}, f32[64,1152]{1,0:T(8,128)S(1)}, u32[]{:S(2)}) copy-start(f32[64,1152]{1,0:T(8,128)S(1)} %get-tuple-element.177) | copy-start | bytes 884740
  88.9 62.0 %copy-start.231 = (f32[64]{0:T(128)}, f32[64]{0:T(128)S(1)}, u32[]{:S(2)}) copy-start(f32[64]{0:T(128)S(1)} %get-tuple-element.136) | copy-start | bytes 772
  89.7 144.7 %copy-start.205 = (f32[64]{0:T(128)}, f32[64]{0:T(128)S(1)}, u32[]{:S(2)}) copy-start(f32[64]{0:T(128)S(1)} %get-tuple-element.138) | copy-start | bytes 772
  161.1 85.1 %copy-start.15 = (f32[64,6912]{1,0:T(8,128)}, f32[64,6912]{1,0:T(8,128)S(1)}, u32[]{:S(2)}) copy-start(f32[64,6912]{1,0:T(8,128)S(1)} %fusion.34) | copy-start | bytes 5308420
  317.9 15.2 %copy-start.274 = (pred[64]{0:T(512)(128)(4,1)S(1)}, pred[64]{0:T(512)(128)(4,1)}, u32[]{:S(2)}) copy-start(pred[64]{0:T(512)(128)(4,1)} %iota_compare_fusion.2) | copy-start | bytes 196
  317.9 17.7 %copy-start.65 = (bf16[128,1152]{1,0:T(8,128)(2,1)S(1)}, bf16[128,1152]{1,0:T(8,128)(2,1)}, u32[]{:S(2)}) copy-start(bf16[128,1152]{1,0:T(8,128)(2,1)} %param.16) | copy-start | bytes 884740
  317.9 18.5 %copy-start.127 = (f32[1152]{0:T(1024)S(1)}, f32[1152]{0:T(1024)}, u32[]{:S(2)}) copy-start(f32[1152]{0:T(1024)} %copy-done.126) | copy-start | bytes 13828
  317.9 19.5 %copy-start.6 = (bf16[1,1152,256]{2,1,0:T(8,128)(2,1)S(1)}, bf16[1,1152,256]{2,1,0:T(8,128)(2,1)}, u32[]{:S(2)}) copy-start(bf16[1,1152,256]{2,1,0:T(8,128)(2,1)} %copy-done.5) | copy-start | bytes 1769476
  326.7 13.4 copy-start.25
  326.7 12.1 copy-start
  328.0 7.6 collective-permute-start
  343.1 9.6 copy-start.1
  379.2 15.8 %copy-start.184 = (f32[256]{0:T(256)S(1)}, f32[256]{0:T(256)}, u32[]{:S(2)}) copy-start(f32[256]{0:T(256)} %copy-done.183) | copy-start | bytes 3076
  379.2 17.7 %copy-start.66 = (bf16[128,1152]{1,0:T(8,128)(2,1)S(1)}, bf16[128,1152]{1,0:T(8,128)(2,1)}, u32[]{:S(2)}) copy-start(bf16[128,1152]{1,0:T(8,128)(2,1)} %param.16) | copy-start | bytes 884740
  379.2 18.5 %copy-start.128 = (f32[1152]{0:T(1024)S(1)}, f32[1152]{0:T(1024)}, u32[]{:S(2)}) copy-start(f32[1152]{0:T(1024)} %copy-done.126) | copy-start | bytes 13828
  388.0 12.2 copy-start.28
  388.0 10.7 copy-start.7
  389.2 7.7 collective-permute-start.1
  447.2 9.6 copy-start.12
  479.1 9.3 copy-start.32
  479.1 10.1 copy-start.271
  479.2 11.5 copy-start.2
  514.0 10.2 collective-permute-start.2
  548.9 9.3 copy-start.34
  549.0 9.3 copy-start.40
  549.0 9.3 copy-start.124
  549.0 9.3 copy-start.246
  549.0 9.3 copy-start.248
  549.0 9.3 copy-start.267
  549.0 11.1 copy-start.266
  549.0 12.4 copy-start.3
  580.8 9.4 collective-permute-start.3
  614.9 9.3 copy-start.36
  615.0 9.3 copy-start.38
  615.0 9.3 copy-start.125
  615.0 11.0 copy-start.261
  615.0 12.4 copy-start.4
  647.9 58.2 %all-gather.29.cloned.1.call-start = ((), (), s32[]{:S(2)}) async-start(), calls=%async_computation.7 | async-start | bytes 2359296 | tf_op jit(solution)/shard_map/all_gather | solution.py:416
  649.0 85.2 %all-gather.31.cloned.1.call-start = ((), (), s32[]{:S(2)}) async-start(), calls=%async_computation.8 | async-start | bytes 2654208 | tf_op jit(solution)/shard_map/all_gather | solution.py:423
  650.0 111.9 %all-gather.27.cloned.1.call-start = ((), (), s32[]{:S(2)}) async-start(), calls=%async_computation.6 | async-start | bytes 2359296 | tf_op jit(solution)/shard_map/all_gather | solution.py:420
  651.9 137.6 %all-gather.41.cloned.1.call-start = ((), (), s32[]{:S(2)}) async-start(), calls=%async_computation.13 | async-start | bytes 2654208 | tf_op jit(solution)/shard_map/all_gather | solution.py:425
  652.9 213.5 %all-gather.39.cloned.1.call-start = ((), (), s32[]{:S(2)}) async-start(), calls=%async_computation.12 | async-start | bytes 15925248 | tf_op jit(solution)/shard_map/all_gather | solution.py:417
  655.2 238.8 %all-gather.33.cloned.1.call-start = ((), (), s32[]{:S(2)}) async-start(), calls=%async_computation.9 | async-start | bytes 2654208 | tf_op jit(solution)/shard_map/all_gather | solution.py:424
  657.2 313.8 %all-gather.35.cloned.1.call-start = ((), (), s32[]{:S(2)}) async-start(), calls=%async_computation.10 | async-start | bytes 15925248 | tf_op jit(solution)/shard_map/all_gather | solution.py:418
  660.6 386.9 %all-gather.37.cloned.1.call-start = ((), (), s32[]{:S(2)}) async-start(), calls=%async_computation.11 | async-start | bytes 15925248 | tf_op jit(solution)/shard_map/all_gather | solution.py:419
  665.5 669.3 %all-reduce.18.cloned.1.call-start = ((), (), s32[]{:S(2)}) async-start(), calls=%async_computation.14 | async-start | bytes 13418496 | tf_op jit(solution)/shard_map/psum | solution.py:442
  894.1 153.4 %copy-start.275 = (bf16[1024,1152]{1,0:T(8,128)(2,1)S(1)}, bf16[1024,1152]{1,0:T(8,128)(2,1)}, u32[]{:S(2)}) copy-start(bf16[1024,1152]{1,0:T(8,128)(2,1)} %all-gather.33.cloned.1.call-done) | copy-start | bytes 7077892
  (233 other events, 752.1 us)
Sparse Core Ops, SparseCore 0:
  9.7 28.5 all-gather.14
  40.0 26.9 all-gather.16
  68.7 82.1 all-gather.18
  152.4 81.9 all-gather.20
  235.9 81.9 all-gather.22
  648.0 31.3 all-gather.24
  681.1 24.9 all-gather.28
  707.8 26.2 all-gather.30
  735.9 25.9 all-gather.26
  763.4 26.0 all-gather.40
  791.8 74.5 all-gather.38
  867.9 26.0 all-gather.32
  896.3 74.5 all-gather.34
  973.1 74.3 all-gather.36
  1053.5 281.2 all-reduce.17
where the time goes:
time: 1360 us
  waiting for transfers between devices  769 us (57%)
  matrix products  266 us (20%)
  blocking collectives  126 us (9%)
  other arithmetic  99.6 us (7%)
  local copies, waits for them, and re-layouts  59.2 us (4%)
  between operations  20.8 us (2%)
  starting transfers between devices  14.6 us (1%)
    psum x1, waiting for transfers between devices, shards(): lax.psum(query_shard.astype(jnp.bfloat16), 'replica').astype(jnp.float32)  230 us
    all_gather x1, waiting for transfers between devices, shards(): lax.all_gather(mixed, 'fsdp', axis=0, tiled=True)  76.9 us
    all_gather x1, waiting for transfers between devices, shards(): lax.all_gather(grad_gate_b, 'fsdp', axis=0, tiled=True)  76.9 us
    all_gather x1, waiting for transfers between devices, shards(): lax.all_gather(up_weight, 'fsdp', axis=2, tiled=True)  73.3 us
    all_gather x1, waiting for transfers between devices, shards(): lax.all_gather(down_weight, 'fsdp', axis=1, tiled=True)  71.8 us
    all_gather x1, waiting for transfers between devices, shards(): lax.all_gather(grad_up_b, 'fsdp', axis=0, tiled=True)  70.1 us
    all_gather x1, waiting for transfers between devices, shards(): lax.all_gather(gate_weight, 'fsdp', axis=2, tiled=True)  61.2 us
    unnamed x2, blocking collectives  47.1 us
  transfers between devices with their start and end apart: 19, of which 14 were waited for; matrix products, arithmetic and copies ran while one was open for 8% of the time, Pallas kernels for 0%

commit v1 on v0

--- a/solution.py
+++ b/solution.py
@@ -291,11 +291,6 @@
     return lax.dot_general(
         left_rows, right_rows, (((0,), (0,)), ((), ())), preferred_element_type=jnp.float32
     )
-
-
-def own_columns(rows_array, fsdp_count, fsdp_index):
-    width = rows_array.shape[1] // fsdp_count
-    return lax.dynamic_slice_in_dim(rows_array, fsdp_index * width, width, 1)
 
 
 def shards(
@@ -409,14 +404,12 @@
         lax.psum_scatter(sum_ffw_pre, "fsdp", scatter_dimension=0, tiled=True),
         lax.psum_scatter(sum_ffw_post, "fsdp", scatter_dimension=0, tiled=True),
     )
-    fsdp_count = lax.axis_size("fsdp")
-    fsdp_index = lax.axis_index("fsdp")
     gathered_rows = (
-        lax.all_gather(normed_rows, "fsdp", axis=0, tiled=True),
-        lax.all_gather(context_rows, "fsdp", axis=0, tiled=True),
-        lax.all_gather(mixed, "fsdp", axis=0, tiled=True),
-        lax.all_gather(grad_gate_b, "fsdp", axis=0, tiled=True),
-        lax.all_gather(grad_up_b, "fsdp", axis=0, tiled=True),
+        lax.all_to_all(normed_rows, "fsdp", split_axis=1, concat_axis=0, tiled=True),
+        lax.all_to_all(context_rows, "fsdp", split_axis=1, concat_axis=0, tiled=True),
+        lax.all_to_all(mixed, "fsdp", split_axis=1, concat_axis=0, tiled=True),
+        lax.all_to_all(grad_gate_b, "fsdp", split_axis=1, concat_axis=0, tiled=True),
+        lax.all_to_all(grad_up_b, "fsdp", split_axis=1, concat_axis=0, tiled=True),
         lax.all_gather(grad_query_b, "fsdp", axis=0, tiled=True),
         lax.all_gather(grad_key_b, "fsdp", axis=0, tiled=True),
         lax.all_gather(grad_value_b, "fsdp", axis=0, tiled=True),
@@ -424,9 +417,7 @@
         lax.all_gather(normed_mid, "fsdp", axis=0, tiled=True),
         lax.all_gather(grad_ffw_b, "fsdp", axis=0, tiled=True),
     )
-    own_parts = tuple(
-        (own_columns(rows_array, fsdp_count, fsdp_index) for rows_array in gathered_rows[:5])
-    )
+    own_parts = gathered_rows[:5]
     full_parts = gathered_rows[5:]
     normed_own, context_own, mixed_own, gate_own, up_own = own_parts
     query_all, key_all, value_all, attn_all, normed_mid_all, ffw_all = full_parts

time: 1360 us -> 1120 us (0.82)
  waiting for transfers between devices: 769 us -> 469 us
  starting transfers between devices: 14.6 us -> 39.6 us
  local copies, waits for them, and re-layouts: 59.2 us -> 82.3 us
  blocking collectives: 126 us -> 145 us
    all_gather x5 -> x0, waiting for transfers between devices: 229 us -> none  [the longest x1 76.9 us: shards(): lax.all_gather(mixed, 'fsdp', axis=0, tiled=True)]
    all_gather x1, waiting for transfers between devices: 28 us -> 0.01 us  [shards(): lax.all_gather(grad_attn_b, 'fsdp', axis=0, tiled=True)]
    all_to_all x0 -> x5, waiting for transfers between devices: none -> 28 us  [the longest x1 20.8 us: shards(): lax.all_to_all(grad_up_b, 'fsdp', split_axis=1, concat_axis=0, tiled=True)]
    all_to_all x0 -> x5, starting transfers between devices: none -> 24.8 us  [the longest x1 5.71 us: shards(): lax.all_to_all(normed_rows, 'fsdp', split_axis=1, concat_axis=0, tiled=True)]
    all_gather x1, waiting for transfers between devices: 24.7 us -> 0.01 us  [shards(): lax.all_gather(grad_query_b, 'fsdp', axis=0, tiled=True)]
    all_gather x1, waiting for transfers between devices: 24.3 us -> 0.02 us  [shards(): lax.all_gather(grad_ffw_b, 'fsdp', axis=0, tiled=True)]
    all_to_all x0 -> x9, local copies, waits for them, and re-layouts: none -> 24 us  [the longest x2 7.16 us: shards(): lax.all_to_all(mixed, 'fsdp', split_axis=1, concat_axis=0, tiled=True)]
    all_gather x1, waiting for transfers between devices: 21.2 us -> 0.01 us  [shards(): lax.all_gather(normed_mid, 'fsdp', axis=0, tiled=True)]
  transfers between devices with their start and end apart: 19 -> 19, of which waited for: 14 -> 9; matrix products, arithmetic and copies ran while one was open for 8% -> 11% of each run, Pallas kernels for 0% -> 0%
where the time goes in v1:
time: 1120 us
  waiting for transfers between devices  469 us (42%)
  matrix products  257 us (23%)
  blocking collectives  145 us (13%)
  other arithmetic  103 us (9%)
  local copies, waits for them, and re-layouts  82.3 us (7%)
  starting transfers between devices  39.6 us (4%)
  between operations  21 us (2%)
    psum x1, waiting for transfers between devices, shards(): lax.psum(query_shard.astype(jnp.bfloat16), 'replica').astype(jnp.float32)  229 us
    all_gather x1, waiting for transfers between devices, shards(): lax.all_gather(up_weight, 'fsdp', axis=2, tiled=True)  73.3 us
    all_gather x1, waiting for transfers between devices, shards(): lax.all_gather(down_weight, 'fsdp', axis=1, tiled=True)  71.8 us
    all_gather x1, waiting for transfers between devices, shards(): lax.all_gather(gate_weight, 'fsdp', axis=2, tiled=True)  61.3 us
    unnamed x2, blocking collectives  48.2 us
    dot_general x3, matrix products, layer_backward(): jnp.dot(grad_ffw_b, down_weight.T, preferred_element_type=jnp.float32)  37.6 us
    dot_general x3, matrix products, layer_forward(): up_rows = jnp.dot(normed_mid, up_weight, preferred_element_type=jnp.float32)  36.3 us
    dot_general x3, matrix products, layer_forward(): jnp.dot(normed_mid, gate_weight, preferred_element_type=jnp.float32)  33.1 us
  transfers between devices with their start and end apart: 19, of which 9 were waited for; matrix products, arithmetic and copies ran while one was open for 11% of the time, Pallas kernels for 0%

profile of v1, /device:TPU:7, one launch (start us, length us, event | category | flops | bytes accessed | tf_op | source)
XLA Modules:
  0.0 1116.5 jit_solution(6455645599492741783)
XLA Ops:
  14.2 24.9 %all-reduce.15 = (bf16[1152]{0:T(1024)(128)(2,1)S(1)}, bf16[256]{0:T(256)(128)(2,1)S(1)}, bf16[256]{0:T(256)(128)(2,1)S(1)}, bf16[1152]{0:T(1024)(128)(2,1)S(1)}...) all-reduce(bf16[1152]{0:T(1024)(128)(2,1)S(1)} %dynamic-update-slic, ...), channel_id=1, replica_groups=mesh['section'=2,'fsdp'=8,'replica'=8] {'fsdp'}, use_global_device_ids=true, to_apply=%add | all-reduce | flops 5120 | bytes 20480
  44.3 17.3 %all_gather.58 = bf16[1,1152,256]{2,1,0:T(8,128)(2,1)S(1)} all-gather(bf16[1,144,256]{2,1,0:T(8,128)(2,1)S(1)} %copy-done.158), channel_id=1, replica_groups=mesh['section'=2,'fsdp'=8,'replica'=8] {'fsdp'}, dimensions={1}, use_global_device_ids=true | all-gather | bytes 663552 | tf_op jit(solution)/shard_map/all_gather | solution.py:319
  61.9 13.4 %all_gather.59 = bf16[1,1152,256]{2,1,0:T(8,128)(2,1)S(1)} all-gather(bf16[1,144,256]{2,1,0:T(8,128)(2,1)S(1)} %copy-done.159), channel_id=1, replica_groups=mesh['section'=2,'fsdp'=8,'replica'=8] {'fsdp'}, dimensions={1}, use_global_device_ids=true | all-gather | bytes 663552 | tf_op jit(solution)/shard_map/all_gather | solution.py:318
  80.2 2.6 fusion.61
  85.9 2.3 multiply_reduce_fusion.26
  89.6 61.3 %all-gather.14.cloned.1.call-done = bf16[1,1152,6912]{1,2,0:T(8,128)(2,1)} async-done(((bf16[1,1152,864]{1,2,0:T(8,128)(2,1)}), bf16[1,1152,6912]{1,2,0:T(8,128)(2,1)}) %all-gather.14.cloned.1.call-update) | async-done | bytes 15925264 | tf_op jit(solution)/shard_map/all_gather | solution.py:325
  150.9 10.2 fusion.34
  161.2 73.3 %all-gather.16.cloned.1.call-done = bf16[1,1152,6912]{1,2,0:T(8,128)(2,1)} async-done(((bf16[1,1152,864]{1,2,0:T(8,128)(2,1)}), bf16[1,1152,6912]{1,2,0:T(8,128)(2,1)}) %all-gather.16.cloned.1.call-update) | async-done | bytes 15925264 | tf_op jit(solution)/shard_map/all_gather | solution.py:326
  234.5 11.7 %multiply_convert_fusion.5 = (bf16[64,6912]{1,0:T(8,128)(2,1)}, f32[64,6912]{1,0:T(8,128)}) fusion(f32[64,6912]{1,0:T(8,128)S(1)} %fusion.34, bf16[1,1152,6912]{1,2,0:T(8,128)(2,1)} %all-gather.16.cloned.1.call-done, f32[64,1152]{1,0:T(8,128)S(1)} %get-tuple-element.82, f32[1152]{0:T(1024)S(1)} %mul.2651, f32[64]{0:T(128)S(1)} %get-tuple-element.138), kind=kOutput, calls=%fused_computation.136 | convolution fusion | flops 1023860736 | bytes 20648704 | tf_op jit(solution)/shard_map/dot_general | solution.py:149
  246.2 71.8 %all-gather.18.cloned.1.call-done = bf16[1,6912,1152]{2,1,0:T(8,128)(2,1)} async-done(((bf16[1,864,1152]{2,1,0:T(8,128)(2,1)}), bf16[1,6912,1152]{2,1,0:T(8,128)(2,1)}) %all-gather.18.cloned.1.call-update) | async-done | bytes 15925264 | tf_op jit(solution)/shard_map/all_gather | solution.py:327
  318.0 8.8 multiply_reduce_fusion.24
  328.0 5.1 collective-permute-start
  333.7 1.8 collective-permute-done
  353.6 11.4 %fusion.32 = f32[64,6912]{1,0:T(8,128)} fusion(bf16[1,1152,6912]{1,2,0:T(8,128)(2,1)} %all-gather.14.cloned.1.call-done, f32[64,1152]{1,0:T(8,128)S(1)} %get-tuple-element.78, f32[1152]{0:T(1024)S(1)} %mul.2651, f32[64]{0:T(128)S(1)} %get-tuple-element.154), kind=kOutput, calls=%fused_computation.32 | convolution fusion | flops 1019437056 | bytes 17994496 | tf_op jit(solution)/shard_map/dot_general | solution.py:148
  365.0 12.2 %multiply_convert_fusion.4 = (bf16[64,6912]{1,0:T(8,128)(2,1)}, f32[64,6912]{1,0:T(8,128)}) fusion(f32[64,6912]{1,0:T(8,128)} %fusion.32, bf16[1,1152,6912]{1,2,0:T(8,128)(2,1)} %all-gather.16.cloned.1.call-done, f32[64,1152]{1,0:T(8,128)S(1)} %get-tuple-element.78, f32[1152]{0:T(1024)S(1)} %mul.2651, f32[64]{0:T(128)} %copy-done.194), kind=kOutput, calls=%fused_computation.135 | convolution fusion | flops 1023860736 | bytes 20648704 | tf_op jit(solution)/shard_map/dot_general | solution.py:149
  377.3 8.8 multiply_reduce_fusion.21
  387.3 5.8 collective-permute-start.1
  415.2 11.5 %fusion.30 = f32[64,6912]{1,0:T(8,128)} fusion(bf16[1,1152,6912]{1,2,0:T(8,128)(2,1)} %all-gather.14.cloned.1.call-done, f32[64,1152]{1,0:T(8,128)S(1)} %get-tuple-element.74, f32[1152]{0:T(1024)S(1)} %mul.2651, f32[64]{0:T(128)S(1)} %get-tuple-element.167), kind=kOutput, calls=%fused_computation.30 | convolution fusion | flops 1019437056 | bytes 17994496 | tf_op jit(solution)/shard_map/dot_general | solution.py:148
  426.7 12.3 %multiply_convert_fusion.3 = (bf16[64,6912]{1,0:T(8,128)(2,1)}, f32[64,6912]{1,0:T(8,128)}) fusion(f32[64,6912]{1,0:T(8,128)} %fusion.30, bf16[1,1152,6912]{1,2,0:T(8,128)(2,1)} %all-gather.16.cloned.1.call-done, f32[64,1152]{1,0:T(8,128)} %copy-done.12, f32[1152]{0:T(1024)S(1)} %mul.2651, f32[64]{0:T(128)} %copy-done.196), kind=kOutput, calls=%fused_computation.134 | convolution fusion | flops 1023860736 | bytes 20648704 | tf_op jit(solution)/shard_map/dot_general | solution.py:149
  439.0 8.8 multiply_reduce_fusion.18
  449.5 12.6 %fusion.89 = (bf16[64,6912]{1,0:T(8,128)(2,1)}, bf16[64,6912]{1,0:T(8,128)(2,1)}) fusion(f32[64,6912]{1,0:T(8,128)} %fusion.30, f32[64,6912]{1,0:T(8,128)} %get-tuple-element.203, bf16[64,1152]{1,0:T(8,128)(2,1)} %get-tuple-element.103, bf16[1,6912,1152]{2,1,0:T(8,128)(2,1)} %all-gather.18.cloned.1.call-done), kind=kOutput, calls=%fused_computation.108 | convolution fusion | flops 1029390336 | bytes 21381120 | tf_op jit(solution)/shard_map/dot_general | solution.py:216
  462.1 8.7 fusion.16
  471.0 9.2 multiply_reduce_fusion.5
  485.7 1.8 fusion.142
  525.0 1.9 multiply_reduce_fusion.1
  526.8 1.9 subtract_convert_fusion.3
  528.8 12.5 %fusion.94 = (bf16[64,6912]{1,0:T(8,128)(2,1)}, bf16[64,6912]{1,0:T(8,128)(2,1)}) fusion(f32[64,6912]{1,0:T(8,128)} %fusion.32, f32[64,6912]{1,0:T(8,128)} %get-tuple-element.191, bf16[64,1152]{1,0:T(8,128)(2,1)} %subtract_convert_fusion.3, bf16[1,6912,1152]{2,1,0:T(8,128)(2,1)} %all-gather.18.cloned.1.call-done), kind=kOutput, calls=%fused_computation.113 | convolution fusion | flops 1029390336 | bytes 21381120 | tf_op jit(solution)/shard_map/dot_general | solution.py:216
  541.3 8.7 fusion.14
  550.0 9.2 multiply_reduce_fusion.4
  565.7 1.9 fusion.143
  591.3 1.9 multiply_reduce_fusion
  593.2 1.9 subtract_convert_fusion.1
  595.1 12.5 %fusion.99 = (bf16[64,6912]{1,0:T(8,128)(2,1)}, bf16[64,6912]{1,0:T(8,128)(2,1)}) fusion(f32[64,6912]{1,0:T(8,128)} %copy-done.15, f32[64,6912]{1,0:T(8,128)} %get-tuple-element.179, bf16[64,1152]{1,0:T(8,128)(2,1)} %subtract_convert_fusion.1, bf16[1,6912,1152]{2,1,0:T(8,128)(2,1)} %all-gather.18.cloned.1.call-done), kind=kOutput, calls=%fused_computation.118 | convolution fusion | flops 1029390336 | bytes 21381120 | tf_op jit(solution)/shard_map/dot_general | solution.py:216
  607.6 8.7 fusion.12
  616.4 9.2 multiply_reduce_fusion.3
  648.5 1.9 fusion.196
  660.7 5.7 all-to-all-start
  666.5 4.1 fusion.101
  670.6 4.5 all_to_all.82
  675.1 2.6 copy.365
  677.8 4.9 all-to-all-start.3
  683.7 3.4 fusion.105
  687.0 4.5 all_to_all.78
  691.6 2.6 copy.363
  694.2 20.8 %all-to-all-done.3 = bf16[128,8,864]{0,2,1:T(8,128)(2,1)} async-done(((bf16[128,8,864]{0,2,1:T(8,128)(2,1)}), bf16[128,8,864]{0,2,1:T(8,128)(2,1)}, u32[]{:S(2)}, u32[]{:S(2)}) %all-to-all-start.3) | async-done | bytes 1769504 | tf_op jit(solution)/shard_map/all_to_all | solution.py:412
  715.0 5.5 all-to-all-start.2
  721.5 4.5 all_to_all.86
  726.1 2.6 copy.367
  728.9 31.8 %all_gather.72 = bf16[1024,256]{1,0:T(8,128)(2,1)S(1)} all-gather(bf16[128,256]{1,0:T(8,128)(2,1)S(1)} %bitcast.773), channel_id=1, replica_groups=mesh['section'=2,'fsdp'=8,'replica'=8] {'fsdp'}, dimensions={0}, use_global_device_ids=true | all-gather | bytes 589824 | tf_op jit(solution)/shard_map/all_gather | solution.py:415
  760.7 13.8 %all_gather.71 = bf16[1024,256]{1,0:T(8,128)(2,1)S(1)} all-gather(bf16[128,256]{1,0:T(8,128)(2,1)S(1)} %bitcast.774), channel_id=1, replica_groups=mesh['section'=2,'fsdp'=8,'replica'=8] {'fsdp'}, dimensions={0}, use_global_device_ids=true | all-gather | bytes 589824 | tf_op jit(solution)/shard_map/all_gather | solution.py:414
  774.5 4.4 all-to-all-start.4
  780.6 2.8 fusion.112
  783.4 6.1 fusion.38
  789.5 5.2 fusion.37
  794.7 7.0 all-to-all-done.4
  801.7 4.3 all-to-all-start.1
  806.3 5.9 fusion.36
  812.4 2.9 fusion.72
  820.4 23.3 %all-reduce.12 = (bf16[1152]{0:T(1024)(128)(2,1)S(1)}, bf16[256]{0:T(256)(128)(2,1)S(1)}, bf16[256]{0:T(256)(128)(2,1)S(1)}, bf16[1152]{0:T(1024)(128)(2,1)S(1)}...) all-reduce(f32[1152]{0:T(1024)S(1)} %get-tuple-element.216, ...), channel_id=2, replica_groups=mesh['section'=2,'fsdp'=8,'replica'=8] {'fsdp'}, use_global_device_ids=true, to_apply=%region_46.47.clone | all-reduce | flops 5120 | bytes 30720
  844.2 20.5 %all-reduce.13 = (bf16[1,144]{1,0:T(2,128)(2,1)S(1)}, bf16[1,32]{1,0:T(2,128)(2,1)S(1)}, bf16[1,32]{1,0:T(2,128)(2,1)S(1)}, bf16[1,144]{1,0:T(2,128)(2,1)S(1)}, ...) all-reduce(bf16[1,144]{1,0:T(2,128)(2,1)S(1)} %broadcast_in_dim.132, ...), channel_id=1, replica_groups=mesh['section'=2,'fsdp'=8,'replica'=8] {'replica'}, use_global_device_ids=true, to_apply=%region_47.48 | all-reduce | flops 640 | bytes 2560 | tf_op jit(solution)/shard_map/psum | solution.py:432
  868.7 229.0 %all-reduce.18.cloned.1.call-done = (bf16[1,144,1024]{2,1,0:T(8,128)(2,1)}, bf16[1,144,256]{2,1,0:T(8,128)(2,1)}, bf16[1,144,256]{2,1,0:T(8,128)(2,1)}, bf16[1,1...) async-done(((bf16[1,144,1024]{2,1,0:T(8,128)(2,1)}, bf16[1,144,256]{2,1,0:T(8,128)(2,1)}, ...) | async-done | bytes 6709264 | tf_op jit(solution)/shard_map/psum | solution.py:433
  1097.7 3.9 broadcast_in_dim.151
  1101.6 2.2 broadcast_in_dim.153
  1103.9 2.2 broadcast_in_dim.155
  (840 shorter events, 184.9 us)
Async XLA Ops:
  7.2 73.0 %all-gather.10.cloned.1.call-start = ((), (), s32[]{:S(2)}) async-start(), calls=%async_computation.5 | async-start | bytes 2654208 | tf_op jit(solution)/shard_map/all_gather | solution.py:317
  7.9 78.0 %all-gather.12.cloned.1.call-start = ((), (), s32[]{:S(2)}) async-start(), calls=%async_computation.6 | async-start | bytes 2654208 | tf_op jit(solution)/shard_map/all_gather | solution.py:322
  8.7 142.3 %all-gather.14.cloned.1.call-start = ((), (), s32[]{:S(2)}) async-start(), calls=%async_computation.7 | async-start | bytes 17915904 | tf_op jit(solution)/shard_map/all_gather | solution.py:325
  9.5 29.7 %copy-start.201 = (s32[2]{0:T(128)S(1)}, s32[2]{0:T(128)}, u32[]{:S(2)}) copy-start(s32[2]{0:T(128)} %param.18) | copy-start | bytes 28
  9.5 34.1 %copy-start.56 = (bf16[128,1152]{1,0:T(8,128)(2,1)S(1)}, bf16[128,1152]{1,0:T(8,128)(2,1)}, u32[]{:S(2)}) copy-start(bf16[128,1152]{1,0:T(8,128)(2,1)} %param.16) | copy-start | bytes 884740
  9.5 34.8 %copy-start.158 = (bf16[1,144,256]{2,1,0:T(8,128)(2,1)S(1)}, bf16[1,144,256]{2,1,0:T(8,128)(2,1)}, u32[]{:S(2)}) copy-start(bf16[1,144,256]{2,1,0:T(8,128)(2,1)} %param.22) | copy-start | bytes 221188
  9.5 224.9 %all-gather.16.cloned.1.call-start = ((), (), s32[]{:S(2)}) async-start(), calls=%async_computation.8 | async-start | bytes 17915904 | tf_op jit(solution)/shard_map/all_gather | solution.py:326
  10.1 51.8 %copy-start.159 = (bf16[1,144,256]{2,1,0:T(8,128)(2,1)S(1)}, bf16[1,144,256]{2,1,0:T(8,128)(2,1)}, u32[]{:S(2)}) copy-start(bf16[1,144,256]{2,1,0:T(8,128)(2,1)} %param.21) | copy-start | bytes 221188
  10.1 307.9 %all-gather.18.cloned.1.call-start = ((), (), s32[]{:S(2)}) async-start(), calls=%async_computation.9 | async-start | bytes 17915904 | tf_op jit(solution)/shard_map/all_gather | solution.py:327
  10.7 769.9 %all-gather.20.cloned.1.call-start = ((), (), s32[]{:S(2)}) async-start(), calls=%async_computation.10 | async-start | bytes 2359296 | tf_op jit(solution)/shard_map/all_gather | solution.py:413
  39.1 41.1 %copy-start.113 = (f32[1152]{0:T(1024)}, f32[1152]{0:T(1024)S(1)}, u32[]{:S(2)}) copy-start(f32[1152]{0:T(1024)S(1)} %mul.2649) | copy-start | bytes 13828
  39.1 44.7 %copy-start.171 = (f32[256]{0:T(256)}, f32[256]{0:T(256)S(1)}, u32[]{:S(2)}) copy-start(f32[256]{0:T(256)S(1)} %convert_element_type.623) | copy-start | bytes 3076
  39.1 40.3 %copy-start.151 = (f32[256]{0:T(256)}, f32[256]{0:T(256)S(1)}, u32[]{:S(2)}) copy-start(f32[256]{0:T(256)S(1)} %convert_element_type.622) | copy-start | bytes 3076
  39.2 49.7 %copy-start.107 = (f32[1152]{0:T(1024)}, f32[1152]{0:T(1024)S(1)}, u32[]{:S(2)}) copy-start(f32[1152]{0:T(1024)S(1)} %mul.2650) | copy-start | bytes 13828
  39.2 40.2 %copy-start.188 = (f32[128]{0:T(128)}, f32[128]{0:T(128)S(1)}, u32[]{:S(2)}) copy-start(f32[128]{0:T(128)S(1)} %multiply_power_fusion) | copy-start | bytes 1540
  44.3 35.9 %copy-start.209 = (f32[64]{0:T(128)}, f32[64]{0:T(128)S(1)}, u32[]{:S(2)}) copy-start(f32[64]{0:T(128)S(1)} %get-tuple-element.132) | copy-start | bytes 772
  61.8 22.9 %copy-start.187 = (bf16[64,256,1]{1,0,2:T(8,128)(2,1)}, bf16[64,256,1]{1,0,2:T(8,128)(2,1)S(1)}, u32[]{:S(2)}) copy-start(bf16[64,256,1]{1,0,2:T(8,128)(2,1)S(1)} %fusion.145) | copy-start | bytes 98308
  88.2 72.9 %copy-start.31 = (f32[64,1152]{1,0:T(8,128)}, f32[64,1152]{1,0:T(8,128)S(1)}, u32[]{:S(2)}) copy-start(f32[64,1152]{1,0:T(8,128)S(1)} %get-tuple-element.177) | copy-start | bytes 884740
  88.8 62.1 %copy-start.212 = (f32[64]{0:T(128)}, f32[64]{0:T(128)S(1)}, u32[]{:S(2)}) copy-start(f32[64]{0:T(128)S(1)} %get-tuple-element.136) | copy-start | bytes 772
  89.6 144.9 %copy-start.192 = (f32[64]{0:T(128)}, f32[64]{0:T(128)S(1)}, u32[]{:S(2)}) copy-start(f32[64]{0:T(128)S(1)} %get-tuple-element.138) | copy-start | bytes 772
  161.1 85.1 %copy-start.15 = (f32[64,6912]{1,0:T(8,128)}, f32[64,6912]{1,0:T(8,128)S(1)}, u32[]{:S(2)}) copy-start(f32[64,6912]{1,0:T(8,128)S(1)} %fusion.34) | copy-start | bytes 5308420
  318.0 15.1 %copy-start.250 = (pred[64]{0:T(512)(128)(4,1)S(1)}, pred[64]{0:T(512)(128)(4,1)}, u32[]{:S(2)}) copy-start(pred[64]{0:T(512)(128)(4,1)} %iota_compare_fusion.2) | copy-start | bytes 196
  318.0 17.6 %copy-start.57 = (bf16[128,1152]{1,0:T(8,128)(2,1)S(1)}, bf16[128,1152]{1,0:T(8,128)(2,1)}, u32[]{:S(2)}) copy-start(bf16[128,1152]{1,0:T(8,128)(2,1)} %param.16) | copy-start | bytes 884740
  318.0 19.0 %copy-start.114 = (f32[1152]{0:T(1024)S(1)}, f32[1152]{0:T(1024)}, u32[]{:S(2)}) copy-start(f32[1152]{0:T(1024)} %copy-done.113) | copy-start | bytes 13828
  318.0 19.1 %copy-start.7 = (bf16[1,1152,256]{2,1,0:T(8,128)(2,1)S(1)}, bf16[1,1152,256]{2,1,0:T(8,128)(2,1)}, u32[]{:S(2)}) copy-start(bf16[1,1152,256]{2,1,0:T(8,128)(2,1)} %copy-done.6) | copy-start | bytes 1769476
  326.8 14.6 %copy-start.23 = (f32[64,1152]{1,0:T(8,128)}, f32[64,1152]{1,0:T(8,128)S(1)}, u32[]{:S(2)}) copy-start(f32[64,1152]{1,0:T(8,128)S(1)} %get-tuple-element.181) | copy-start | bytes 884740
  326.8 12.0 %copy-start.152 = (f32[256]{0:T(256)S(1)}, f32[256]{0:T(256)}, u32[]{:S(2)}) copy-start(f32[256]{0:T(256)} %copy-done.151) | copy-start | bytes 3076
  326.8 12.5 %copy-start.189 = (f32[128]{0:T(128)S(1)}, f32[128]{0:T(128)}, u32[]{:S(2)}) copy-start(f32[128]{0:T(128)} %copy-done.188) | copy-start | bytes 1540
  326.8 13.3 %copy-start = (bf16[1,1152,1024]{2,1,0:T(8,128)(2,1)S(1)}, bf16[1,1152,1024]{2,1,0:T(8,128)(2,1)}, u32[]{:S(2)}) copy-start(bf16[1,1152,1024]{2,1,0:T(8,128)(2,1)} %all-gather.10.cloned.1.call-done) | copy-start | bytes 7077892
  328.0 7.6 collective-permute-start
  377.3 15.8 %copy-start.172 = (f32[256]{0:T(256)S(1)}, f32[256]{0:T(256)}, u32[]{:S(2)}) copy-start(f32[256]{0:T(256)} %copy-done.171) | copy-start | bytes 3076
  377.3 17.7 %copy-start.58 = (bf16[128,1152]{1,0:T(8,128)(2,1)S(1)}, bf16[128,1152]{1,0:T(8,128)(2,1)}, u32[]{:S(2)}) copy-start(bf16[128,1152]{1,0:T(8,128)(2,1)} %param.16) | copy-start | bytes 884740
  377.3 19.0 %copy-start.115 = (f32[1152]{0:T(1024)S(1)}, f32[1152]{0:T(1024)}, u32[]{:S(2)}) copy-start(f32[1152]{0:T(1024)} %copy-done.113) | copy-start | bytes 13828
  377.3 19.1 %copy-start.8 = (bf16[1,1152,256]{2,1,0:T(8,128)(2,1)S(1)}, bf16[1,1152,256]{2,1,0:T(8,128)(2,1)}, u32[]{:S(2)}) copy-start(bf16[1,1152,256]{2,1,0:T(8,128)(2,1)} %copy-done.6) | copy-start | bytes 1769476
  386.1 10.7 copy-start.25
  386.1 12.1 %copy-start.153 = (f32[256]{0:T(256)S(1)}, f32[256]{0:T(256)}, u32[]{:S(2)}) copy-start(f32[256]{0:T(256)} %copy-done.151) | copy-start | bytes 3076
  386.1 12.6 %copy-start.190 = (f32[128]{0:T(128)S(1)}, f32[128]{0:T(128)}, u32[]{:S(2)}) copy-start(f32[128]{0:T(128)} %copy-done.188) | copy-start | bytes 1540
  387.3 7.7 collective-permute-start.1
  439.0 9.6 copy-start.13
  470.9 9.3 copy-start.28
  470.9 10.1 copy-start.246
  470.9 11.5 %copy-start.3 = (bf16[1,1024,1152]{2,1,0:T(8,128)(2,1)S(1)}, bf16[1,1024,1152]{2,1,0:T(8,128)(2,1)}, u32[]{:S(2)}) copy-start(bf16[1,1024,1152]{2,1,0:T(8,128)(2,1)} %all-gather.12.cloned.1.call-done) | copy-start | bytes 7077892
  514.9 10.1 collective-permute-start.2
  550.0 9.3 copy-start.29
  550.0 9.3 copy-start.34
  550.0 11.1 copy-start.243
  550.0 12.4 %copy-start.4 = (bf16[1,1024,1152]{2,1,0:T(8,128)(2,1)S(1)}, bf16[1,1024,1152]{2,1,0:T(8,128)(2,1)}, u32[]{:S(2)}) copy-start(bf16[1,1024,1152]{2,1,0:T(8,128)(2,1)} %all-gather.12.cloned.1.call-done) | copy-start | bytes 7077892
  582.0 9.3 collective-permute-start.3
  616.3 9.3 copy-start.30
  616.3 9.3 copy-start.32
  616.3 11.1 copy-start.239
  616.4 12.4 %copy-start.5 = (bf16[1,1024,1152]{2,1,0:T(8,128)(2,1)S(1)}, bf16[1,1024,1152]{2,1,0:T(8,128)(2,1)}, u32[]{:S(2)}) copy-start(bf16[1,1024,1152]{2,1,0:T(8,128)(2,1)} %all-gather.12.cloned.1.call-done) | copy-start | bytes 7077892
  642.3 141.1 %all-gather.24.cloned.1.call-start = ((), (), s32[]{:S(2)}) async-start(), calls=%async_computation.12 | async-start | bytes 2654208 | tf_op jit(solution)/shard_map/all_gather | solution.py:417
  645.8 160.5 %all-gather.26.cloned.1.call-start = ((), (), s32[]{:S(2)}) async-start(), calls=%async_computation.13 | async-start | bytes 2654208 | tf_op jit(solution)/shard_map/all_gather | solution.py:418
  660.7 17.0 %all-to-all-start = ((bf16[128,8,144]{0,2,1:T(8,128)(2,1)}), bf16[128,8,144]{0,2,1:T(8,128)(2,1)S(1)}, u32[]{:S(2)}, u32[]{:S(2)}) async-start(bf16[128,8,144]{0,2,1:T(8,128)(2,1)} %copy.348), calls=%async_computation | async-start | bytes 589824 | tf_op jit(solution)/shard_map/all_to_all | solution.py:408
  677.8 37.2 %all-to-all-start.3 = ((bf16[128,8,864]{0,2,1:T(8,128)(2,1)}), bf16[128,8,864]{0,2,1:T(8,128)(2,1)}, u32[]{:S(2)}, u32[]{:S(2)}) async-start(bf16[128,8,864]{0,2,1:T(8,128)(2,1)} %copy.365), calls=%async_computation.3 | async-start | bytes 3538944 | tf_op jit(solution)/shard_map/all_to_all | solution.py:412
  682.7 129.7 %all-gather.22.cloned.1.call-start = ((), (), s32[]{:S(2)}) async-start(), calls=%async_computation.11 | async-start | bytes 2654208 | tf_op jit(solution)/shard_map/all_gather | solution.py:416
  694.2 26.3 %copy-start.77 = (bf16[1,64,4,256]{3,1,2,0:T(8,128)(2,1)S(1)}, bf16[1,64,4,256]{3,1,2,0:T(8,128)(2,1)}, u32[]{:S(2)}) copy-start(bf16[1,64,4,256]{3,1,2,0:T(8,128)(2,1)} %copy-done.76) | copy-start | bytes 393220
  694.2 26.3 %copy-start.79 = (bf16[1,64,4,256]{3,1,2,0:T(8,128)(2,1)S(1)}, bf16[1,64,4,256]{3,1,2,0:T(8,128)(2,1)}, u32[]{:S(2)}) copy-start(bf16[1,64,4,256]{3,1,2,0:T(8,128)(2,1)} %copy-done.78) | copy-start | bytes 393220
  694.2 26.3 %copy-start.81 = (bf16[1,64,4,256]{3,1,2,0:T(8,128)(2,1)S(1)}, bf16[1,64,4,256]{3,1,2,0:T(8,128)(2,1)}, u32[]{:S(2)}) copy-start(bf16[1,64,4,256]{3,1,2,0:T(8,128)(2,1)} %copy-done.80) | copy-start | bytes 393220
  715.0 59.5 %all-to-all-start.2 = ((bf16[128,8,864]{0,2,1:T(8,128)(2,1)}), bf16[128,8,864]{0,2,1:T(8,128)(2,1)}, u32[]{:S(2)}, u32[]{:S(2)}) async-start(bf16[128,8,864]{0,2,1:T(8,128)(2,1)} %copy.363), calls=%async_computation.2 | async-start | bytes 3538944 | tf_op jit(solution)/shard_map/all_to_all | solution.py:411
  774.5 27.2 %all-to-all-start.4 = ((bf16[128,8,864]{0,2,1:T(8,128)(2,1)}), bf16[128,8,864]{0,2,1:T(8,128)(2,1)}, u32[]{:S(2)}, u32[]{:S(2)}) async-start(bf16[128,8,864]{0,2,1:T(8,128)(2,1)} %copy.367), calls=%async_computation.4 | async-start | bytes 3538944 | tf_op jit(solution)/shard_map/all_to_all | solution.py:410
  801.7 10.8 all-to-all-start.1
  805.9 291.7 %all-reduce.18.cloned.1.call-start = ((), (), s32[]{:S(2)}) async-start(), calls=%async_computation.14 | async-start | bytes 13418496 | tf_op jit(solution)/shard_map/psum | solution.py:433
  (209 other events, 659.8 us)
Sparse Core Ops, SparseCore 0:
  9.7 28.5 all-gather.9
  40.0 26.9 all-gather.11
  68.6 82.2 all-gather.13
  152.5 81.9 all-gather.15
  236.0 81.9 all-gather.17
  642.4 30.9 all-gather.19
  675.1 36.1 all-gather.23
  712.9 35.7 all-gather.25
  751.0 28.6 all-gather.21
  815.5 282.0 all-reduce.17
